TPU v7x, 32 devices: a whole 2x2x4 slice. The times are simulated.
32 devices in a mesh: lat: 4 (over y, x), lon: 8 (over z, core).
Axes of the slice: x: 2, y: 2, z: 4, core: 2. Of those that a mesh axis runs over, the one named last changes fastest.
Arguments:
- prior: float32 [64, 128, 1024], P(None, 'lat', 'lon'), may hold values from 0.1 to 1
- habitat: bfloat16 [32, 128, 1024], P(None, 'lat', 'lon'), may hold values from -6 to 6
- kappa: float32 [128, 1024], P('lat', 'lon'), may hold values from 0.03 to 0.24
- ocean_mask: int32 [128, 1024], P('lat', 'lon'), may hold values 0 or 1
- profiles: float32 [256, 32], P('lon'), may hold values from -6 to 6
- tag_ids: int32 [256], P('lon'), may hold values from 0 to 63
Outputs:
- posterior: float32 [64, 128, 1024], P(None, 'lat', 'lon')
- log_evidence: float32 [64], replicated
All inputs are finite; a program needn't handle non-finite values. No bound on the sum of `ocean_mask` on one device may be relied on, other than what follows from the above.
Results may differ from a plain program's by a relative error of at most 0.0003.
Values sent between devices are 32-bit elements; how exact they have to be, the bound alone decides.
A program may use at most 64 MiB of HBM per device.

v0:
```python
import jax
import jax.numpy as jnp
from jax import lax
from jax.sharding import PartitionSpec as P

reach_weights = (0.4, 0.3, 0.2, 0.1)
misfit_scale = 8.0


def with_halo(block, sides, width, periodic):
    for axis, dim in sides:
        count = lax.axis_size(axis)
        forward = [(i, i + 1) for i in range(count - 1)]
        if periodic:
            forward.append((count - 1, 0))
        backward = [(target, source) for source, target in forward]
        low = lax.ppermute(
            lax.slice_in_dim(block, block.shape[dim] - width, None, axis=dim), axis, forward
        )
        high = lax.ppermute(lax.slice_in_dim(block, 0, width, axis=dim), axis, backward)
        block = jnp.concatenate([low, block, high], axis=dim)
    return block


def cross_step(extended, coeff, ocean):
    rows = extended.shape[1] - 8
    cols = extended.shape[2] - 8
    center = extended[:, 4 : 4 + rows, 4 : 4 + cols]
    accum = -4.0 * center
    for reach in range(1, 5):
        weight = reach_weights[reach - 1]
        accum = accum + weight * (
            extended[:, 4 + reach : 4 + reach + rows, 4 : 4 + cols]
            + extended[:, 4 - reach : 4 - reach + rows, 4 : 4 + cols]
            + extended[:, 4 : 4 + rows, 4 + reach : 4 + reach + cols]
            + extended[:, 4 : 4 + rows, 4 - reach : 4 - reach + cols]
        )
    return (center + coeff * accum) * ocean


def lat_narrow(field):
    return with_halo(field, (("lat", 1),), 4, False)


def lon_narrow(field):
    return with_halo(field, (("lon", 2),), 4, True)


def rims_narrow(field):
    return lon_narrow(lat_narrow(field))


def body(prior, habitat, kappa, ocean_mask, profiles, tag_ids):
    ocean = ocean_mask.astype(jnp.float32)
    tag_count = prior.shape[0]
    onehot = (tag_ids[:, None] == jnp.arange(tag_count, dtype=jnp.int32)[None, :]).astype(
        jnp.float32
    )
    local_first = jnp.dot(onehot.T, profiles, precision=lax.Precision.HIGHEST)
    local_second = jnp.dot(
        onehot.T, jnp.sum(profiles * profiles, 1), precision=lax.Precision.HIGHEST
    )
    local_count = jnp.sum(onehot, 0)
    first_moment, second_moment, count = lax.psum((local_first, local_second, local_count), "lon")
    field = prior * ocean
    for sweep in range(2):
        field = cross_step(rims_narrow(field), kappa, ocean)
    habfloat = habitat.astype(jnp.float32)
    habsquare = jnp.sum(habfloat * habfloat, 0)
    crossed = jnp.einsum("tl,lab->tab", first_moment, habfloat, precision=lax.Precision.HIGHEST)
    misfit = second_moment[:, None, None] - 2.0 * crossed + count[:, None, None] * habsquare[None]
    levels = habitat.shape[0]
    updated = field * jnp.exp(-misfit / (misfit_scale * levels))
    local_total = jnp.sum(updated, axis=(1, 2))
    total = lax.psum(local_total, ("lat", "lon"))
    cells = jnp.float32(
        prior.shape[1] * prior.shape[2] * lax.axis_size("lat") * lax.axis_size("lon")
    )
    return (updated * (cells / total)[:, None, None], jnp.log(total / cells))


def solution(mesh):
    placed = (
        P(None, "lat", "lon"),
        P(None, "lat", "lon"),
        P("lat", "lon"),
        P("lat", "lon"),
        P("lon", None),
        P("lon"),
    )
    return jax.shard_map(
        body, mesh=mesh, in_specs=placed, out_specs=(P(None, "lat", "lon"), P()), check_vma=False
    )
```

profile of v0, /device:TPU:0, one launch (start us, length us, event | category | flops | bytes accessed | tf_op | source)
XLA Modules:
  0.0 125.5 jit_solution(17771117196643437231)
XLA Ops:
  1.4 1.9 %copy_multiply_fusion = f32[64,32,128]{2,0,1:T(8,128)S(1)} fusion(f32[64,32,128]{2,1,0:T(8,128)} %param.6, f32[32,128]{1,0:T(8,128)S(1)} %convert_element_type.9), kind=kLoop, calls=%fused_computation.100 | loop fusion | flops 262144 | bytes 2113536 | tf_op jit(solution)/shard_map/mul | solution.py:65
  3.2 1.3 %collective-permute-start = (f32[64,4,128]{2,0,1:T(8,128)S(1)}, f32[64,4,128]{2,0,1:T(8,128)S(1)}, u32[]{:S(2)}, u32[]{:S(2)}) collective-permute-start(f32[64,4,128]{2,0,1:T(8,128)S(1)} %get-tuple-element.21), channel_id=1, source_target_pairs={{8,0},{16,8},{24,16},{9,1},{17,9},{25,17},{10,2},{18,10},{26,18},{... | collective-permute-start | bytes 393224 | tf_op jit(solution)/shard_map/ppermute | solution.py:20
  4.5 5.5 %collective-permute-start.1 = (f32[64,4,128]{2,0,1:T(8,128)S(1)}, f32[64,4,128]{2,0,1:T(8,128)S(1)}, u32[]{:S(2)}, u32[]{:S(2)}) collective-permute-start(f32[64,4,128]{2,0,1:T(8,128)S(1)} %get-tuple-element.22), channel_id=1, source_target_pairs={{0,8},{8,16},{16,24},{1,9},{9,17},{17,25},{2,10},{10,18},{18,26},{... | collective-permute-start | bytes 393224 | tf_op jit(solution)/shard_map/ppermute | solution.py:17
  10.1 0.8 fusion.62
  11.6 1.2 collective-permute-done.1
  12.9 1.5 %fusion.67 = (f32[64,40,4]{2,0,1:T(8,128)}, f32[64,40,4]{2,0,1:T(8,128)S(1)}) fusion(f32[64,40,128]{2,0,1:T(8,128)S(1)} %pad_maximum_fusion.2), kind=kLoop, calls=%fused_computation.116 | loop fusion | bytes 163840 | tf_op jit(solution)/shard_map/slice | solution.py:20
  14.4 1.8 %copy.23 = f32[64,40,4]{0,1,2:T(8,128)S(1)} copy(f32[64,40,4]{2,0,1:T(8,128)} %get-tuple-element.17) | data formatting | bytes 81920 | tf_op jit(solution)/shard_map/slice | solution.py:20
  16.2 2.2 %collective-permute-start.2 = (f32[64,40,4]{0,1,2:T(8,128)S(1)}, f32[64,40,4]{0,1,2:T(8,128)S(1)}, u32[]{:S(2)}, u32[]{:S(2)}) collective-permute-start(f32[64,40,4]{0,1,2:T(8,128)S(1)} %copy.23), channel_id=1, source_target_pairs={{1,0},{2,1},{3,2},{4,3},{5,4},{6,5},{7,6},{0,7},{9,8},{10,9},{11,1... | collective-permute-start | bytes 122888 | tf_op jit(solution)/shard_map/ppermute | solution.py:20
  19.5 1.3 %collective-permute-done.2 = f32[64,40,4]{0,1,2:T(8,128)S(1)} collective-permute-done((f32[64,40,4]{0,1,2:T(8,128)S(1)}, f32[64,40,4]{0,1,2:T(8,128)S(1)}, u32[]{:S(2)}, u32[]{:S(2)}) %collective-permute-start.2) | collective-permute-done | bytes 40992 | tf_op jit(solution)/shard_map/ppermute | solution.py:20
  21.3 3.2 %collective-permute-done.3 = f32[64,40,4]{0,1,2:T(8,128)S(1)} collective-permute-done((f32[64,40,4]{0,1,2:T(8,128)S(1)}, f32[64,40,4]{0,1,2:T(8,128)S(1)}, u32[]{:S(2)}, u32[]{:S(2)}) %collective-permute-start.3) | collective-permute-done | bytes 40992 | tf_op jit(solution)/shard_map/ppermute | solution.py:17
  24.6 1.6 %copy.26 = f32[64,40,4]{2,0,1:T(8,128)} copy(f32[64,40,4]{0,1,2:T(8,128)S(1)} %collective-permute-done.3) | data formatting | bytes 81920 | tf_op jit(solution)/shard_map/ppermute | solution.py:17
  26.1 2.2 %pad_maximum_fusion = (f32[64,40,132]{2,0,1:T(8,128)S(1)}, f32[64,40,132]{2,0,1:T(8,128)S(1)}) fusion(f32[64,40,4]{2,0,1:T(8,128)S(1)} %copy.24, f32[64,4,128]{2,0,1:T(8,128)S(1)} %collective-permute-done, f32[64,32,128]{2,0,1:T(8,128)S(1)} %copy_multiply_fusion, f32[64,4,128]{2,0,1:T(8,128)S(1)} %collective-permute-done.1, f32[64,40,4]{2,0,1:T(8,128)} %copy.26), kind=kLoop, calls=%fused_computation | loop fusion | flops 2027520 | bytes 4096000 | tf_op jit(solution)/shard_map/concatenate | solution.py:21
  28.4 3.1 %fusion.40 = f32[64,32,128]{2,0,1:T(8,128)S(1)} fusion(f32[64,32,128]{2,0,1:T(8,128)S(1)} %copy_multiply_fusion, f32[64,4,128]{2,0,1:T(8,128)} %copy-done, f32[64,4,128]{2,0,1:T(8,128)S(1)} %collective-permute-done, f32[64,40,132]{2,0,1:T(8,128)S(1)} %get-tuple-element.16, f32[64,40,132]{2,0,1:T(8,128)S(1)} %get-tuple-element.15, ...), kind=kLoop, calls=%fused_computation.72 | loop fusion | flops 8388608 | bytes 10780672 | tf_op jit(solution)/shard_map/mul | solution.py:38
  31.5 1.3 %collective-permute-start.4 = (f32[64,4,128]{2,0,1:T(8,128)S(1)}, f32[64,4,128]{2,0,1:T(8,128)S(1)}, u32[]{:S(2)}, u32[]{:S(2)}) collective-permute-start(f32[64,4,128]{2,0,1:T(8,128)S(1)} %get-tuple-element.19), channel_id=1, source_target_pairs={{8,0},{16,8},{24,16},{9,1},{17,9},{25,17},{10,2},{18,10},{26,18},{... | collective-permute-start | bytes 393224 | tf_op jit(solution)/shard_map/ppermute | solution.py:20
  32.8 5.0 %collective-permute-start.5 = (f32[64,4,128]{2,0,1:T(8,128)S(1)}, f32[64,4,128]{2,0,1:T(8,128)S(1)}, u32[]{:S(2)}, u32[]{:S(2)}) collective-permute-start(f32[64,4,128]{2,0,1:T(8,128)S(1)} %get-tuple-element.20), channel_id=1, source_target_pairs={{0,8},{8,16},{16,24},{1,9},{9,17},{17,25},{2,10},{10,18},{18,26},{... | collective-permute-start | bytes 393224 | tf_op jit(solution)/shard_map/ppermute | solution.py:17
  38.6 1.1 collective-permute-done.4
  40.4 1.5 %fusion.66 = (f32[64,40,4]{2,0,1:T(8,128)}, f32[64,40,4]{2,0,1:T(8,128)S(1)}) fusion(f32[64,40,128]{2,0,1:T(8,128)S(1)} %pad_maximum_fusion.3), kind=kLoop, calls=%fused_computation.115 | loop fusion | bytes 163840 | tf_op jit(solution)/shard_map/slice | solution.py:20
  42.0 1.8 %copy.27 = f32[64,40,4]{0,1,2:T(8,128)S(1)} copy(f32[64,40,4]{2,0,1:T(8,128)} %get-tuple-element.13) | data formatting | bytes 81920 | tf_op jit(solution)/shard_map/slice | solution.py:20
  44.9 29.7 %all-reduce = (f32[64]{0:T(128)}, f32[64]{0:T(128)}, f32[64,32]{0,1:T(8,128)}) all-reduce(f32[64]{0:T(128)S(1)} %copy-done.10, f32[64]{0:T(128)S(1)} %convolution_bitcast_fusion, f32[64,32]{0,1:T(8,128)S(1)} %copy-done.9), channel_id=1, replica_groups=mesh['lat'=4,'lon'=8] {'lon'}, use_global_device_ids=true, to_apply=%region_4.0 | all-reduce | flops 2176 | bytes 17408 | tf_op jit(solution)/shard_map/psum | solution.py:64
  75.1 1.6 %copy.30 = f32[64,40,4]{2,0,1:T(8,128)} copy(f32[64,40,4]{0,1,2:T(8,128)S(1)} %collective-permute-done.7) | data formatting | bytes 81920 | tf_op jit(solution)/shard_map/ppermute | solution.py:17
  76.7 2.3 %pad_maximum_fusion.1 = (f32[64,40,132]{2,0,1:T(8,128)S(1)}, f32[64,40,132]{2,0,1:T(8,128)S(1)}) fusion(f32[64,40,4]{2,0,1:T(8,128)S(1)} %copy.28, f32[64,4,128]{2,0,1:T(8,128)S(1)} %collective-permute-done.4, f32[64,32,128]{2,0,1:T(8,128)S(1)} %fusion.40, f32[64,4,128]{2,0,1:T(8,128)S(1)} %collective-permute-done.5, f32[64,40,4]{2,0,1:T(8,128)} %copy.30), kind=kLoop, calls=%fused_computation.2 | loop fusion | flops 2027520 | bytes 4096000 | tf_op jit(solution)/shard_map/concatenate | solution.py:21
  79.0 3.5 %fusion.70 = (f32[64]{0:T(128)S(1)}, f32[64,32,128]{2,0,1:T(8,128)S(1)}) fusion(f32[32,128]{1,0:T(8,128)S(1)} %copy-done.6, f32[64]{0:T(128)S(1)} %copy-done.14, bf16[32,32,128]{2,1,0:T(8,128)(2,1)S(1)} %copy-done.3, f32[64,32]{0,1:T(8,128)S(1)} %copy-done.11, f32[64]{0:T(128)S(1)} %copy-done.15, f32[32,128]{1,0:T(8,128)S(1)} %convert_element_type.9, ...), kind=kOutput, calls=%fused_computation.119 | convolution fusion | flops 111148992 | bytes 11068160 | tf_op jit(solution)/shard_map/tl,lab->tab/dot_general | solution.py:70
  82.6 40.6 %psum.31 = f32[64]{0:T(128)S(1)} all-reduce(f32[64]{0:T(128)S(1)} %get-tuple-element.25), channel_id=1, replica_groups=mesh['lat'=4,'lon'=8] {'lat','lon'}, use_global_device_ids=true, to_apply=%region_7.0 | all-reduce | flops 64 | bytes 512 | tf_op jit(solution)/shard_map/psum | solution.py:75
  123.9 1.6 %copy.32 = f32[64,32,128]{2,1,0:T(8,128)} copy(f32[64,32,128]{2,0,1:T(8,128)S(1)} %broadcast_multiply_fusion) | data formatting | bytes 2097152
  (54 shorter events, 7.0 us)
Async XLA Ops:
  1.4 8.7 %copy-start.7 = (f32[32,32]{1,0:T(8,128)S(1)}, f32[32,32]{1,0:T(8,128)}, u32[]{:S(2)}) copy-start(f32[32,32]{1,0:T(8,128)} %param.10) | copy-start | bytes 12292
  1.4 8.7 %copy-start.12 = (s32[32]{0:T(128)S(1)}, s32[32]{0:T(128)}, u32[]{:S(2)}) copy-start(s32[32]{0:T(128)} %param.11) | copy-start | bytes 388
  3.2 8.4 %collective-permute-start = (f32[64,4,128]{2,0,1:T(8,128)S(1)}, f32[64,4,128]{2,0,1:T(8,128)S(1)}, u32[]{:S(2)}, u32[]{:S(2)}) collective-permute-start(f32[64,4,128]{2,0,1:T(8,128)S(1)} %get-tuple-element.21), channel_id=1, source_target_pairs={{8,0},{16,8},{24,16},{9,1},{17,9},{25,17},{10,2},{18,10},{26,18},{... | collective-permute-start | bytes 393224 | tf_op jit(solution)/shard_map/ppermute | solution.py:20
  4.5 8.2 %collective-permute-start.1 = (f32[64,4,128]{2,0,1:T(8,128)S(1)}, f32[64,4,128]{2,0,1:T(8,128)S(1)}, u32[]{:S(2)}, u32[]{:S(2)}) collective-permute-start(f32[64,4,128]{2,0,1:T(8,128)S(1)} %get-tuple-element.22), channel_id=1, source_target_pairs={{0,8},{8,16},{16,24},{1,9},{9,17},{17,25},{2,10},{10,18},{18,26},{... | collective-permute-start | bytes 393224 | tf_op jit(solution)/shard_map/ppermute | solution.py:17
  12.8 13.3 %copy-start = (f32[64,4,128]{2,0,1:T(8,128)}, f32[64,4,128]{2,0,1:T(8,128)S(1)}, u32[]{:S(2)}) copy-start(f32[64,4,128]{2,0,1:T(8,128)S(1)} %collective-permute-done.1) | copy-start | bytes 393220
  16.2 4.7 %collective-permute-start.2 = (f32[64,40,4]{0,1,2:T(8,128)S(1)}, f32[64,40,4]{0,1,2:T(8,128)S(1)}, u32[]{:S(2)}, u32[]{:S(2)}) collective-permute-start(f32[64,40,4]{0,1,2:T(8,128)S(1)} %copy.23), channel_id=1, source_target_pairs={{1,0},{2,1},{3,2},{4,3},{5,4},{6,5},{7,6},{0,7},{9,8},{10,9},{11,1... | collective-permute-start | bytes 122888 | tf_op jit(solution)/shard_map/ppermute | solution.py:20
  18.9 5.7 %collective-permute-start.3 = (f32[64,40,4]{0,1,2:T(8,128)S(1)}, f32[64,40,4]{0,1,2:T(8,128)S(1)}, u32[]{:S(2)}, u32[]{:S(2)}) collective-permute-start(f32[64,40,4]{0,1,2:T(8,128)S(1)} %copy.25), channel_id=1, source_target_pairs={{0,1},{1,2},{2,3},{3,4},{4,5},{5,6},{6,7},{7,0},{8,9},{9,10},{10,1... | collective-permute-start | bytes 122888 | tf_op jit(solution)/shard_map/ppermute | solution.py:17
  26.1 2.2 %copy-start.4 = (f32[32,128]{1,0:T(8,128)S(1)}, f32[32,128]{1,0:T(8,128)}, u32[]{:S(2)}) copy-start(f32[32,128]{1,0:T(8,128)} %param.8) | copy-start | bytes 49156
  28.4 9.5 %copy-start.8 = (f32[32,32]{1,0:T(8,128)S(1)}, f32[32,32]{1,0:T(8,128)}, u32[]{:S(2)}) copy-start(f32[32,32]{1,0:T(8,128)} %param.10) | copy-start | bytes 12292
  28.4 9.6 %copy-start.2 = (bf16[32,32,128]{2,1,0:T(8,128)(2,1)S(1)}, bf16[32,32,128]{2,1,0:T(8,128)(2,1)}, u32[]{:S(2)}) copy-start(bf16[32,32,128]{2,1,0:T(8,128)(2,1)} %param.7) | copy-start | bytes 786436
  31.5 8.2 %collective-permute-start.4 = (f32[64,4,128]{2,0,1:T(8,128)S(1)}, f32[64,4,128]{2,0,1:T(8,128)S(1)}, u32[]{:S(2)}, u32[]{:S(2)}) collective-permute-start(f32[64,4,128]{2,0,1:T(8,128)S(1)} %get-tuple-element.19), channel_id=1, source_target_pairs={{8,0},{16,8},{24,16},{9,1},{17,9},{25,17},{10,2},{18,10},{26,18},{... | collective-permute-start | bytes 393224 | tf_op jit(solution)/shard_map/ppermute | solution.py:20
  32.8 7.5 %collective-permute-start.5 = (f32[64,4,128]{2,0,1:T(8,128)S(1)}, f32[64,4,128]{2,0,1:T(8,128)S(1)}, u32[]{:S(2)}, u32[]{:S(2)}) collective-permute-start(f32[64,4,128]{2,0,1:T(8,128)S(1)} %get-tuple-element.20), channel_id=1, source_target_pairs={{0,8},{8,16},{16,24},{1,9},{9,17},{17,25},{2,10},{10,18},{18,26},{... | collective-permute-start | bytes 393224 | tf_op jit(solution)/shard_map/ppermute | solution.py:17
  40.3 36.4 %copy-start.1 = (f32[64,4,128]{2,0,1:T(8,128)}, f32[64,4,128]{2,0,1:T(8,128)S(1)}, u32[]{:S(2)}) copy-start(f32[64,4,128]{2,0,1:T(8,128)S(1)} %collective-permute-done.5) | copy-start | bytes 393220
  41.9 2.8 %copy-start.13 = (s32[32]{0:T(128)S(1)}, s32[32]{0:T(128)}, u32[]{:S(2)}) copy-start(s32[32]{0:T(128)} %param.11) | copy-start | bytes 388
  42.0 3.0 %copy-start.9 = (f32[64,32]{0,1:T(8,128)S(1)}, f32[64,32]{0,1:T(8,128)}, u32[]{:S(2)}) copy-start(f32[64,32]{0,1:T(8,128)} %fusion.62) | copy-start | bytes 24580
  42.0 3.0 %copy-start.10 = (f32[64]{0:T(128)S(1)}, f32[64]{0:T(128)}, u32[]{:S(2)}) copy-start(f32[64]{0:T(128)} %convert_reduce_fusion) | copy-start | bytes 772
  43.8 30.9 %collective-permute-start.6 = (f32[64,40,4]{0,1,2:T(8,128)S(1)}, f32[64,40,4]{0,1,2:T(8,128)S(1)}, u32[]{:S(2)}, u32[]{:S(2)}) collective-permute-start(f32[64,40,4]{0,1,2:T(8,128)S(1)} %copy.27), channel_id=1, source_target_pairs={{1,0},{2,1},{3,2},{4,3},{5,4},{6,5},{7,6},{0,7},{9,8},{10,9},{11,1... | collective-permute-start | bytes 122888 | tf_op jit(solution)/shard_map/ppermute | solution.py:20
  44.6 30.6 %collective-permute-start.7 = (f32[64,40,4]{0,1,2:T(8,128)S(1)}, f32[64,40,4]{0,1,2:T(8,128)S(1)}, u32[]{:S(2)}, u32[]{:S(2)}) collective-permute-start(f32[64,40,4]{0,1,2:T(8,128)S(1)} %copy.29), channel_id=1, source_target_pairs={{0,1},{1,2},{2,3},{3,4},{4,5},{5,6},{6,7},{7,0},{8,9},{9,10},{10,1... | collective-permute-start | bytes 122888 | tf_op jit(solution)/shard_map/ppermute | solution.py:17
  76.7 2.3 %copy-start.3 = (bf16[32,32,128]{2,1,0:T(8,128)(2,1)S(1)}, bf16[32,32,128]{2,1,0:T(8,128)(2,1)}, u32[]{:S(2)}) copy-start(bf16[32,32,128]{2,1,0:T(8,128)(2,1)} %param.7) | copy-start | bytes 786436
  76.7 2.3 %copy-start.5 = (f32[32,128]{1,0:T(8,128)S(1)}, f32[32,128]{1,0:T(8,128)}, u32[]{:S(2)}) copy-start(f32[32,128]{1,0:T(8,128)} %param.8) | copy-start | bytes 49156
  76.7 2.3 %copy-start.6 = (f32[32,128]{1,0:T(8,128)S(1)}, f32[32,128]{1,0:T(8,128)}, u32[]{:S(2)}) copy-start(f32[32,128]{1,0:T(8,128)} %multiply_reduce_fusion) | copy-start | bytes 49156
  76.7 2.3 %copy-start.11 = (f32[64,32]{0,1:T(8,128)S(1)}, f32[64,32]{0,1:T(8,128)}, u32[]{:S(2)}) copy-start(f32[64,32]{0,1:T(8,128)} %get-tuple-element.10) | copy-start | bytes 24580
  76.7 2.3 %copy-start.14 = (f32[64]{0:T(128)S(1)}, f32[64]{0:T(128)}, u32[]{:S(2)}) copy-start(f32[64]{0:T(128)} %get-tuple-element.8) | copy-start | bytes 772
  76.7 2.3 %copy-start.15 = (f32[64]{0:T(128)S(1)}, f32[64]{0:T(128)}, u32[]{:S(2)}) copy-start(f32[64]{0:T(128)} %get-tuple-element.9) | copy-start | bytes 772
where the time goes:
time: 127 us; the launch traced here: 126 us
  blocking collectives  70.4 us (55%)
  starting transfers between devices  15.9 us (13%)
  local copies, waits for them, and re-layouts  13.3 us (10%)
  other arithmetic  12.4 us (10%)
  waiting for transfers between devices  8.17 us (6%)
  matrix products  4.45 us (4%)
    psum x1, blocking collectives, body(): total = lax.psum(local_total, ('lat', 'lon'))  40.6 us
    psum x1, blocking collectives, body(): lax.psum((local_first, local_second, local_count), 'lon')  29.7 us
    ppermute x4, starting transfers between devices, with_halo(): lax.ppermute(lax.slice_in_dim(block, block.shape[dim] - width, None, axis...  10.8 us
    slice x6, local copies, waits for them, and re-layouts, with_halo(): lax.slice_in_dim(block, 0, width, axis=dim)  6.69 us
    ppermute x4, starting transfers between devices, with_halo(): lax.ppermute(lax.slice_in_dim(block, 0, width, axis=dim), axis, backward)  5.16 us
    ppermute x4, waiting for transfers between devices, with_halo(): lax.ppermute(lax.slice_in_dim(block, block.shape[dim] - width, None, axis...  5.04 us
    concatenate x4, other arithmetic, with_halo(): block = jnp.concatenate([low, block, high], axis=dim)  4.65 us
    dot_general x1, matrix products, body(): jnp.einsum('tl,lab->tab', first_moment, habfloat, precision=lax.Precision...  3.51 us
  transfers between devices with their start and end apart: 8, of which 6 were waited for; matrix products, arithmetic and copies ran while one was open for 3% of the time, Pallas kernels for 0%

commit v1 on v0

v1 whole, which is shorter than its diff:
```python
import functools

import jax
import jax.numpy as jnp
from jax import lax
from jax.experimental import pallas as pl
from jax.experimental.pallas import tpu as pltpu
from jax.sharding import PartitionSpec as P

MESH = pl.DeviceIdType.MESH
HIGHEST = lax.Precision.HIGHEST
misfit_scale = 8.0
DEEP = 8
REACH = 4


def spread(rows):
    count, lanes = rows.shape
    return jnp.broadcast_to(rows[:, None, :], (count, 8, lanes)).reshape(count * 8, lanes)


def kernel(
    dims, prior3, prior2, hab2, kappa, mask, profiles, ids, out2, logev,
    pr, hb, hf, ext, one, lik, ak, aux_lo, aux_hi, bulk_lo, bulk_hi, kb, khb,
    px, px_left, px_right, he, ce, h1, mom, acc, tot1, tot2,
    loc_sem, mom_s, mom_r, px_s, px_r, aux_s, aux_r, bulk_s, bulk_r, cor_s, cor_r,
    t1_s, t1_r, t2_s, t2_r,
):
    n_lat, n_lon, tags, levels, rows, lanes = dims
    groups = tags // 8
    erows = rows + 2 * DEEP
    hrows = rows + 2 * REACH
    half = tags // 2
    lat, lon = lax.axis_index("lat"), lax.axis_index("lon")
    has_lo, has_hi = lat > 0, lat < n_lat - 1
    left, right = lax.rem(lon + n_lon - 1, n_lon), lax.rem(lon + 1, n_lon)

    own_prior = pltpu.make_async_copy(prior2, pr, loc_sem.at[0])
    own_hab = pltpu.make_async_copy(hab2, hb, loc_sem.at[1])
    own_prior.start()
    own_hab.start()

    barrier = pltpu.get_barrier_semaphore()
    for k in range(1, n_lon):
        pl.semaphore_signal(
            barrier, inc=1, device_id={"lon": lax.rem(lon + k, n_lon)}, device_id_type=MESH
        )
    for k in range(1, n_lat):
        pl.semaphore_signal(
            barrier, inc=1, device_id={"lat": lax.rem(lat + k, n_lat)}, device_id_type=MESH
        )

    def remote(src, dst, send, recv, where):
        return pltpu.make_async_remote_copy(
            src_ref=src, dst_ref=dst, send_sem=send, recv_sem=recv, device_id=where,
            device_id_type=MESH,
        )

    lane = lax.broadcasted_iota(jnp.int32, (8, lanes), 1)
    ocean = mask[...].astype(jnp.float32)
    ko = kappa[...] * ocean
    ak[0] = ocean
    ak[1] = ko
    prof = profiles[...]
    local = prof.shape[0]
    squares = jnp.sum(prof * prof, 1, keepdims=True)
    table = jnp.concatenate(
        [
            prof,
            squares,
            jnp.ones((local, 1), jnp.float32),
            jnp.zeros((local, 128 - levels - 2), jnp.float32),
        ],
        axis=1,
    )
    onehot = (
        lax.broadcasted_iota(jnp.int32, (tags, local), 0) == ids[...]
    ).astype(jnp.float32)
    sums = jnp.dot(onehot, table, precision=HIGHEST, preferred_element_type=jnp.float32)
    mom[lon] = sums[:half] + pltpu.roll(sums[half:], 64, 1)
    folded = pltpu.roll(ko, DEEP, 1)
    folded = jnp.where(lax.broadcasted_iota(jnp.int32, (rows, lanes), 1) < 16, folded, 0.0)
    for step in (16, 32, 64):
        folded = folded + pltpu.roll(folded, step, 1)
    px[pl.ds(rows * 8, rows), :] = folded

    pl.semaphore_wait(barrier, n_lon - 1 + n_lat - 1)

    to_hi_aux = remote(
        ak.at[:, rows - DEEP : rows, :], aux_lo, aux_s.at[0], aux_r.at[0], {"lat": lat + 1}
    )
    to_lo_aux = remote(ak.at[:, 0:DEEP, :], aux_hi, aux_s.at[1], aux_r.at[1], {"lat": lat - 1})

    def to_hi(g):
        return remote(
            prior3.at[pl.ds(g * 8, 8), rows - DEEP : rows, :],
            bulk_lo.at[pl.ds(g * 8, 8)],
            bulk_s.at[0, g],
            bulk_r.at[0, g],
            {"lat": lat + 1},
        )

    def to_lo(g):
        return remote(
            prior3.at[pl.ds(g * 8, 8), 0:DEEP, :],
            bulk_hi.at[pl.ds(g * 8, 8)],
            bulk_s.at[1, g],
            bulk_r.at[1, g],
            {"lat": lat - 1},
        )

    moment_copies = []
    for k in range(1, n_lon):
        copy = remote(
            mom.at[lon], mom.at[lon], mom_s.at[k - 1], mom_r.at[k - 1],
            {"lon": lax.rem(lon + k, n_lon)},
        )
        copy.start()
        moment_copies.append(copy)

    early = groups // 2

    @pl.when(has_hi)
    def _():
        to_hi_aux.start()
        for g in range(early):
            to_hi(g).start()

    @pl.when(has_lo)
    def _():
        to_lo_aux.start()
        for g in range(early):
            to_lo(g).start()

    @pl.when(jnp.logical_not(has_lo))
    def _():
        bulk_lo[...] = jnp.zeros_like(bulk_lo)
        aux_lo[...] = jnp.zeros_like(aux_lo)
        he[0 : REACH * 8, :] = jnp.zeros((REACH * 8, lanes), jnp.float32)

    @pl.when(jnp.logical_not(has_hi))
    def _():
        bulk_hi[...] = jnp.zeros_like(bulk_hi)
        aux_hi[...] = jnp.zeros_like(aux_hi)
        he[(REACH + rows) * 8 : hrows * 8, :] = jnp.zeros((REACH * 8, lanes), jnp.float32)

    own_prior.wait()

    def pack(a, carry):
        wet = jnp.broadcast_to(ak[0, pl.ds(a, 1), :], (8, lanes))
        packed = jnp.zeros((8, lanes), jnp.float32)
        for g in range(groups):
            value = pr[pl.ds(g * 8 * rows + a, 8, stride=rows), :] * wet
            ext[pl.ds(pl.multiple_of((g * erows + DEEP + a) * 8, 8), 8), :] = value
            turned = pltpu.roll(value, (DEEP + 16 * g) % lanes, 1)
            packed = jnp.where((lane >= 16 * g) & (lane < 16 * g + 16), turned, packed)
        px[pl.ds(pl.multiple_of(a * 8, 8), 8), :] = packed
        return carry

    lax.fori_loop(0, rows, pack, 0, unroll=2)

    to_right = remote(px, px_left, px_s.at[0], px_r.at[0], {"lon": right})
    to_left = remote(px, px_right, px_s.at[1], px_r.at[1], {"lon": left})
    to_right.start()
    to_left.start()

    own_hab.wait()
    hf[...] = hb[...].astype(jnp.float32)
    for copy in moment_copies:
        copy.wait()
    total_moments = mom[0]
    for k in range(1, n_lon):
        total_moments = total_moments + mom[k]
    moments = jnp.concatenate([total_moments, pltpu.roll(total_moments, 64, 1)], axis=0)
    tag_lane = lax.broadcasted_iota(jnp.int32, (tags, lanes), 1)
    second = jnp.broadcast_to(moments[:, levels : levels + 1], (tags, lanes))
    count = jnp.broadcast_to(moments[:, levels + 1 : levels + 2], (tags, lanes))
    first = jnp.where(tag_lane < levels, moments, 0.0)
    top = first.astype(jnp.bfloat16).astype(jnp.float32)
    rest = first - top
    middle = rest.astype(jnp.bfloat16).astype(jnp.float32)
    bottom = (rest - middle).astype(jnp.bfloat16).astype(jnp.float32)
    split = (top + pltpu.roll(middle, levels, 1) + pltpu.roll(bottom, 2 * levels, 1)).astype(
        jnp.bfloat16
    )
    pad = jnp.zeros((lanes - 3 * levels, lanes), jnp.bfloat16)

    def likelihood(a, carry):
        field = hf[pl.ds(a, levels, stride=rows), :]
        square = jnp.sum(field * field, 0, keepdims=True)
        narrow = field.astype(jnp.bfloat16)
        crossed = jnp.dot(
            split,
            jnp.concatenate([narrow, narrow, narrow, pad], axis=0),
            preferred_element_type=jnp.float32,
        )
        misfit = second - 2.0 * crossed + count * square
        value = jnp.exp(misfit * (-1.0 / (misfit_scale * levels)))
        for g in range(groups):
            lik[pl.ds(pl.multiple_of((g * rows + a) * 8, 8), 8), :] = value[g * 8 : g * 8 + 8]
        return carry

    lax.fori_loop(0, rows, likelihood, 0, unroll=2)

    to_right.wait()
    to_left.wait()
    low_side = lax.rem(lax.broadcasted_iota(jnp.int32, (64, lanes), 1), 16) < 8
    for b in range(rows // 8):
        he[(REACH + 8 * b) * 8 : (REACH + 8 * b + 8) * 8, :] = jnp.where(
            low_side, px_left[b * 64 : b * 64 + 64, :], px_right[b * 64 : b * 64 + 64, :]
        )
    low_rows = lax.rem(lax.broadcasted_iota(jnp.int32, (rows, lanes), 1), 16) < 8
    ko_side = jnp.where(
        low_rows, px_left[rows * 8 : rows * 9, :], px_right[rows * 8 : rows * 9, :]
    )
    khb[...] = spread(ko_side)

    cor_hi = remote(
        he.at[rows * 8 : (rows + REACH) * 8, :], he.at[0 : REACH * 8, :],
        cor_s.at[0], cor_r.at[0], {"lat": lat + 1},
    )
    cor_lo = remote(
        he.at[REACH * 8 : 2 * REACH * 8, :], he.at[(REACH + rows) * 8 : hrows * 8, :],
        cor_s.at[1], cor_r.at[1], {"lat": lat - 1},
    )

    @pl.when(has_hi)
    def _():
        cor_hi.start()
        for g in range(early, groups):
            to_hi(g).start()

    @pl.when(has_lo)
    def _():
        cor_lo.start()
        for g in range(early, groups):
            to_lo(g).start()

    @pl.when(has_lo)
    def _():
        to_hi_aux.wait_recv()
        cor_hi.wait_recv()

    @pl.when(has_hi)
    def _():
        to_lo_aux.wait_recv()
        cor_lo.wait_recv()

    kb[0 : REACH * 8, :] = spread(aux_lo[1])[REACH * 8 :]
    kb[REACH * 8 : (REACH + rows) * 8, :] = spread(ak[1])
    kb[(REACH + rows) * 8 :, :] = spread(aux_hi[1])[: REACH * 8]

    def lon_sum(low, high):
        total = pltpu.roll(low, REACH, 1) + pltpu.roll(high, lanes - REACH, 1)
        for d in range(1, REACH):
            total = total + (5.0 - d) * (pltpu.roll(low, d, 1) + pltpu.roll(high, lanes - d, 1))
        return total

    def lat_sum(ref, at):
        total = ref[pl.ds(at - 8 * REACH, 64), :] + ref[pl.ds(at + 8 * REACH, 64), :]
        for d in range(1, REACH):
            total = total + (5.0 - d) * (
                ref[pl.ds(at - 8 * d, 64), :] + ref[pl.ds(at + 8 * d, 64), :]
            )
        return total

    def across(field):
        from_low = jnp.where(low_side, field, 0.0)
        from_high = jnp.where(low_side, 0.0, field)
        low, high = pltpu.roll(from_low, REACH, 1), pltpu.roll(from_high, lanes - REACH, 1)
        for d in range(1, REACH):
            low = low + (5.0 - d) * pltpu.roll(from_low, d, 1)
            high = high + (5.0 - d) * pltpu.roll(from_high, lanes - d, 1)
        return jnp.where(low_side, high, low)

    for b in range(hrows // 8):
        ce[b * 64 : b * 64 + 64, :] = across(he[b * 64 : b * 64 + 64, :])

    for b in range(rows // 8):
        at = (REACH + 8 * b) * 8
        side = he[at : at + 64, :]
        inner = px[b * 64 : b * 64 + 64, :]
        z_left = jnp.where(low_side, side, inner)
        z_right = jnp.where(low_side, inner, side)
        along = jnp.where(low_side, lon_sum(z_left, z_left), lon_sum(z_right, z_right))
        h1[b * 64 : b * 64 + 64, :] = across(
            side
            + khb[b * 64 : b * 64 + 64, :] * (0.1 * (along + lat_sum(he, at)) - 4.0 * side)
        )

    weights = [
        (
            jnp.concatenate([jnp.where(lane >= d, 5.0 - d, 0.0)] * 8, axis=0),
            jnp.concatenate([jnp.where(lane < lanes - d, 5.0 - d, 0.0)] * 8, axis=0),
        )
        for d in range(1, REACH + 1)
    ]
    at_edge = jnp.concatenate([(lane < REACH) | (lane >= lanes - REACH)] * 8, axis=0)
    low_flat = bulk_lo.reshape(tags * DEEP, lanes)
    high_flat = bulk_hi.reshape(tags * DEEP, lanes)
    acc[...] = jnp.zeros_like(acc)

    def sweep(center, sides, shift, coeff, ref, at):
        along = jnp.where(at_edge, pltpu.roll(sides, shift, 1), 0.0) + lat_sum(ref, at)
        for d in range(1, REACH + 1):
            up, down = weights[d - 1]
            along = along + up * pltpu.roll(center, d, 1) + down * pltpu.roll(center, lanes - d, 1)
        return center + coeff * (0.1 * along - 4.0 * center)

    def group(g, carry):
        @pl.when(has_lo)
        def _():
            to_hi(g).wait_recv()

        @pl.when(has_hi)
        def _():
            to_lo(g).wait_recv()

        base = g * erows * 8
        for a in range(DEEP):
            ext[pl.ds(pl.multiple_of(base + a * 8, 8), 8), :] = low_flat[
                pl.ds(g * 64 + a, 8, stride=DEEP), :
            ] * jnp.broadcast_to(aux_lo[0, a : a + 1, :], (8, lanes))
            ext[pl.ds(pl.multiple_of(base + (DEEP + rows + a) * 8, 8), 8), :] = high_flat[
                pl.ds(g * 64 + a, 8, stride=DEEP), :
            ] * jnp.broadcast_to(aux_hi[0, a : a + 1, :], (8, lanes))
        shift = lax.rem(lanes - DEEP - 16 * g + lanes, lanes)
        for b in range(hrows // 8):
            at = pl.multiple_of(base + (REACH + 8 * b) * 8, 8)
            one[b * 64 : b * 64 + 64, :] = sweep(
                ext[pl.ds(at, 64), :],
                ce[b * 64 : b * 64 + 64, :],
                shift,
                kb[b * 64 : b * 64 + 64, :],
                ext,
                at,
            )
        partial = jnp.zeros((8, lanes), jnp.float32)
        for b in range(rows // 8):
            at = (REACH + 8 * b) * 8
            here = pl.ds(pl.multiple_of(g * rows * 8 + b * 64, 8), 64)
            updated = (
                sweep(
                    one[at : at + 64, :],
                    h1[b * 64 : b * 64 + 64, :],
                    shift,
                    kb[at : at + 64, :],
                    one,
                    at,
                )
                * lik[here, :]
            )
            lik[here, :] = updated
            partial = partial + jnp.sum(updated.reshape(8, 8, lanes), 0)
        acc[pl.ds(pl.multiple_of(g * 8, 8), 8), :] = partial
        return carry

    lax.fori_loop(0, groups, group, 0)

    row = lax.dot_general(
        jnp.ones((8, lanes), jnp.float32), acc[...], (((1,), (1,)), ((), ())),
        precision=HIGHEST, preferred_element_type=jnp.float32,
    )
    tot1[lon] = row[0:1]
    copies = []
    for k in range(1, n_lon):
        copy = remote(
            tot1.at[lon], tot1.at[lon], t1_s.at[k - 1], t1_r.at[k - 1],
            {"lon": lax.rem(lon + k, n_lon)},
        )
        copy.start()
        copies.append(copy)
    for copy in copies:
        copy.wait()
    total = tot1[0]
    for k in range(1, n_lon):
        total = total + tot1[k]
    tot2[lat] = total
    copies = []
    for k in range(1, n_lat):
        copy = remote(
            tot2.at[lat], tot2.at[lat], t2_s.at[k - 1], t2_r.at[k - 1],
            {"lat": lax.rem(lat + k, n_lat)},
        )
        copy.start()
        copies.append(copy)
    for copy in copies:
        copy.wait()
    total = tot2[0]
    for k in range(1, n_lat):
        total = total + tot2[k]
    cells = float(n_lat * n_lon * rows * lanes)
    logev[...] = jnp.log(total[:, :tags] / cells)
    first_row = lax.broadcasted_iota(jnp.int32, (8, lanes), 0) == 0
    column = lax.dot_general(
        jnp.where(first_row, jnp.broadcast_to(total, (8, lanes)), 0.0),
        jnp.ones((8, lanes), jnp.float32),
        (((0,), (0,)), ((), ())),
        precision=HIGHEST, preferred_element_type=jnp.float32,
    )
    acc[...] = cells / column

    def finish(a, carry):
        for g in range(groups):
            out2[pl.ds(g * 8 * rows + a, 8, stride=rows), :] = (
                lik[pl.ds(pl.multiple_of((g * rows + a) * 8, 8), 8), :]
                * acc[g * 8 : g * 8 + 8, :]
            )
        return carry

    lax.fori_loop(0, rows, finish, 0, unroll=2)

    @pl.when(has_hi)
    def _():
        to_hi_aux.wait_send()
        cor_hi.wait_send()
        for g in range(groups):
            to_hi(g).wait_send()

    @pl.when(has_lo)
    def _():
        to_lo_aux.wait_send()
        cor_lo.wait_send()
        for g in range(groups):
            to_lo(g).wait_send()


def body(n_lat, n_lon, prior, habitat, kappa, ocean_mask, profiles, tag_ids):
    tags, rows, lanes = prior.shape
    levels = habitat.shape[0]
    groups = tags // 8
    erows, hrows = rows + 2 * DEEP, rows + 2 * REACH
    f32 = jnp.float32
    flat = (tags * rows, lanes)
    vmem = pl.BlockSpec(memory_space=pltpu.VMEM)
    hbm = pl.BlockSpec(memory_space=pl.ANY)
    dma = pltpu.SemaphoreType.DMA
    posterior, logev = pl.pallas_call(
        functools.partial(kernel, (n_lat, n_lon, tags, levels, rows, lanes)),
        name="filter_step",
        out_shape=(jax.ShapeDtypeStruct(flat, f32), jax.ShapeDtypeStruct((1, tags), f32)),
        in_specs=[hbm, hbm, hbm, vmem, vmem, vmem, vmem],
        out_specs=(vmem, vmem),
        scratch_shapes=[
            pltpu.VMEM(flat, f32),
            pltpu.VMEM((levels * rows, lanes), habitat.dtype),
            pltpu.VMEM((levels * rows, lanes), f32),
            pltpu.VMEM((groups * erows * 8, lanes), f32),
            pltpu.VMEM((hrows * 8, lanes), f32),
            pltpu.VMEM((groups * rows * 8, lanes), f32),
            pltpu.VMEM((2, rows, lanes), f32),
            pltpu.VMEM((2, DEEP, lanes), f32),
            pltpu.VMEM((2, DEEP, lanes), f32),
            pltpu.VMEM((tags, DEEP, lanes), f32),
            pltpu.VMEM((tags, DEEP, lanes), f32),
            pltpu.VMEM((hrows * 8, lanes), f32),
            pltpu.VMEM((rows * 8, lanes), f32),
            pltpu.VMEM((rows * 9, lanes), f32),
            pltpu.VMEM((rows * 9, lanes), f32),
            pltpu.VMEM((rows * 9, lanes), f32),
            pltpu.VMEM((hrows * 8, lanes), f32),
            pltpu.VMEM((hrows * 8, lanes), f32),
            pltpu.VMEM((rows * 8, lanes), f32),
            pltpu.VMEM((n_lon, tags // 2, lanes), f32),
            pltpu.VMEM((lanes, lanes), f32),
            pltpu.VMEM((n_lon, 1, lanes), f32),
            pltpu.VMEM((n_lat, 1, lanes), f32),
            dma((2,)),
            dma((n_lon - 1,)),
            dma((n_lon - 1,)),
            dma((2,)),
            dma((2,)),
            dma((2,)),
            dma((2,)),
            dma((2, groups)),
            dma((2, groups)),
            dma((2,)),
            dma((2,)),
            dma((n_lon - 1,)),
            dma((n_lon - 1,)),
            dma((n_lat - 1,)),
            dma((n_lat - 1,)),
        ],
        compiler_params=pltpu.CompilerParams(collective_id=0, has_side_effects=True),
    )(
        prior,
        prior.reshape(flat),
        habitat.reshape(levels * rows, lanes),
        kappa,
        ocean_mask,
        profiles,
        tag_ids[None, :],
    )
    return posterior.reshape(prior.shape), logev[0]


def solution(mesh):
    placed = (
        P(None, "lat", "lon"),
        P(None, "lat", "lon"),
        P("lat", "lon"),
        P("lat", "lon"),
        P("lon", None),
        P("lon"),
    )
    return jax.shard_map(
        functools.partial(body, mesh.shape["lat"], mesh.shape["lon"]),
        mesh=mesh,
        in_specs=placed,
        out_specs=(P(None, "lat", "lon"), P()),
        check_vma=False,
    )
```

time: 127 us -> 41.4 us (0.33); the launches traced: 126 us -> 41.2 us
  blocking collectives: 70.4 us -> 0 us
  Pallas kernels: 0 us -> 37.8 us
  starting transfers between devices: 15.9 us -> 0 us
  other arithmetic: 12.4 us -> 0 us
  local copies, waits for them, and re-layouts: 13.3 us -> 2.78 us
  waiting for transfers between devices: 8.17 us -> 0 us
  matrix products: 4.45 us -> 0 us
    psum x2 -> x0, blocking collectives: 70.4 us -> none  [the longest x1 40.6 us: body(): total = lax.psum(local_total, ('lat', 'lon'))]
    pallas_call x0 -> x1, Pallas kernels: none -> 37.8 us  [body(): pl.pallas_call(functools.partial(kernel, (n_lat, n_lon, tags, levels, row...]
    ppermute x8 -> x0, starting transfers between devices: 15.9 us -> none  [the longest x4 10.8 us: with_halo(): lax.ppermute(lax.slice_in_dim(block, block.shape[dim] - width, None, axis...]
    ppermute x8 -> x0, waiting for transfers between devices: 8.17 us -> none  [the longest x4 5.04 us: with_halo(): lax.ppermute(lax.slice_in_dim(block, block.shape[dim] - width, None, axis...]
    slice x8 -> x0, local copies, waits for them, and re-layouts: 7.58 us -> none  [the longest x6 6.69 us: with_halo(): lax.slice_in_dim(block, 0, width, axis=dim)]
    mul x3 -> x0, other arithmetic: 5.15 us -> none  [the longest x1 3.1 us: cross_step(): return (center + coeff * accum) * ocean]
    concatenate x4 -> x0, other arithmetic: 4.65 us -> none  [with_halo(): block = jnp.concatenate([low, block, high], axis=dim)]
    dot_general x3 -> x0, matrix products: 4.45 us -> none  [the longest x1 3.51 us: body(): jnp.einsum('tl,lab->tab', first_moment, habfloat, precision=lax.Precision...]
  transfers between devices with their start and end apart: 8 -> 0, of which waited for: 6 -> 0; matrix products, arithmetic and copies ran while one was open for 3% -> 0% of each run, Pallas kernels for 0% -> 0%
where the time goes in v1:
time: 41.4 us; the launch traced here: 41.2 us
  Pallas kernels  37.8 us (91%)
  local copies, waits for them, and re-layouts  2.78 us (7%)
  between operations  0.65 us (2%)
    pallas_call x1, Pallas kernels, body(): pl.pallas_call(functools.partial(kernel, (n_lat, n_lon, tags, levels, row...  37.8 us
    unnamed x4, local copies, waits for them, and re-layouts  2.78 us

profile of v1, /device:TPU:0, one launch (start us, length us, event | category | flops | bytes accessed | tf_op | source)
XLA Modules:
  0.0 41.2 jit_solution(16858965156014804864)
XLA Ops:
  0.6 37.8 %filter_step.1 = (f32[2048,128]{1,0:T(8,128)}, f32[1,64]{1,0:T(1,128)}) custom-call(f32[64,32,128]{2,1,0:T(8,128)} %prior3.1, f32[2048,128]{1,0:T(8,128)} %bitcast.5, bf16[1024,128]{1,0:T(8,128)(2,1)} %bitcast.7, f32[32,128]{1,0:T(8,128)} %kappa.1, s32[32,128]{1,0:T(8,128)} %mask.1, f32[32,32]{1,0:T(8,128)} %profiles.1, s32[1,32]{1,0:T(1,128)} %bitcast.8), custom_call_target="tpu_custom_call" | custom-call | tf_op jit(solution)/shard_map/filter_step/pallas_call | solution.py:438
  38.4 0.0 copy-start
  38.4 2.3 %copy.10 = f32[64,32,128]{2,1,0:T(8,128)} copy(f32[64,32,128]{2,1,0:T(8,128)} %bitcast.6) | data formatting | bytes 2097152
  40.7 0.0 copy-done
  40.7 0.5 %copy.11 = f32[64]{0:T(128)} copy(f32[64]{0:T(128)S(1)} %bitcast.9) | data formatting | bytes 512
Async XLA Ops:
  38.4 2.3 %copy-start = (f32[1,64]{1,0:T(1,128)S(1)}, f32[1,64]{1,0:T(1,128)}, u32[]{:S(2)}) copy-start(f32[1,64]{1,0:T(1,128)} %get-tuple-element.5) | copy-start | bytes 772

commit v2 on v1

--- a/solution.py
+++ b/solution.py
@@ -84,66 +84,6 @@
         folded = folded + pltpu.roll(folded, step, 1)
     px[pl.ds(rows * 8, rows), :] = folded
 
-    pl.semaphore_wait(barrier, n_lon - 1 + n_lat - 1)
-
-    to_hi_aux = remote(
-        ak.at[:, rows - DEEP : rows, :], aux_lo, aux_s.at[0], aux_r.at[0], {"lat": lat + 1}
-    )
-    to_lo_aux = remote(ak.at[:, 0:DEEP, :], aux_hi, aux_s.at[1], aux_r.at[1], {"lat": lat - 1})
-
-    def to_hi(g):
-        return remote(
-            prior3.at[pl.ds(g * 8, 8), rows - DEEP : rows, :],
-            bulk_lo.at[pl.ds(g * 8, 8)],
-            bulk_s.at[0, g],
-            bulk_r.at[0, g],
-            {"lat": lat + 1},
-        )
-
-    def to_lo(g):
-        return remote(
-            prior3.at[pl.ds(g * 8, 8), 0:DEEP, :],
-            bulk_hi.at[pl.ds(g * 8, 8)],
-            bulk_s.at[1, g],
-            bulk_r.at[1, g],
-            {"lat": lat - 1},
-        )
-
-    moment_copies = []
-    for k in range(1, n_lon):
-        copy = remote(
-            mom.at[lon], mom.at[lon], mom_s.at[k - 1], mom_r.at[k - 1],
-            {"lon": lax.rem(lon + k, n_lon)},
-        )
-        copy.start()
-        moment_copies.append(copy)
-
-    early = groups // 2
-
-    @pl.when(has_hi)
-    def _():
-        to_hi_aux.start()
-        for g in range(early):
-            to_hi(g).start()
-
-    @pl.when(has_lo)
-    def _():
-        to_lo_aux.start()
-        for g in range(early):
-            to_lo(g).start()
-
-    @pl.when(jnp.logical_not(has_lo))
-    def _():
-        bulk_lo[...] = jnp.zeros_like(bulk_lo)
-        aux_lo[...] = jnp.zeros_like(aux_lo)
-        he[0 : REACH * 8, :] = jnp.zeros((REACH * 8, lanes), jnp.float32)
-
-    @pl.when(jnp.logical_not(has_hi))
-    def _():
-        bulk_hi[...] = jnp.zeros_like(bulk_hi)
-        aux_hi[...] = jnp.zeros_like(aux_hi)
-        he[(REACH + rows) * 8 : hrows * 8, :] = jnp.zeros((REACH * 8, lanes), jnp.float32)
-
     own_prior.wait()
 
     def pack(a, carry):
@@ -159,10 +99,151 @@
 
     lax.fori_loop(0, rows, pack, 0, unroll=2)
 
+    pl.semaphore_wait(barrier, n_lon - 1 + n_lat - 1)
+
     to_right = remote(px, px_left, px_s.at[0], px_r.at[0], {"lon": right})
     to_left = remote(px, px_right, px_s.at[1], px_r.at[1], {"lon": left})
     to_right.start()
     to_left.start()
+
+    moment_copies = []
+    for k in range(1, n_lon):
+        copy = remote(
+            mom.at[lon], mom.at[lon], mom_s.at[k - 1], mom_r.at[k - 1],
+            {"lon": lax.rem(lon + k, n_lon)},
+        )
+        copy.start()
+        moment_copies.append(copy)
+
+    to_hi_aux = remote(
+        ak.at[:, rows - DEEP : rows, :], aux_lo, aux_s.at[0], aux_r.at[0], {"lat": lat + 1}
+    )
+    to_lo_aux = remote(ak.at[:, 0:DEEP, :], aux_hi, aux_s.at[1], aux_r.at[1], {"lat": lat - 1})
+
+    def to_hi(g):
+        return remote(
+            prior3.at[pl.ds(g * 8, 8), rows - DEEP : rows, :],
+            bulk_lo.at[pl.ds(g * 8, 8)],
+            bulk_s.at[0, g],
+            bulk_r.at[0, g],
+            {"lat": lat + 1},
+        )
+
+    def to_lo(g):
+        return remote(
+            prior3.at[pl.ds(g * 8, 8), 0:DEEP, :],
+            bulk_hi.at[pl.ds(g * 8, 8)],
+            bulk_s.at[1, g],
+            bulk_r.at[1, g],
+            {"lat": lat - 1},
+        )
+
+    early = groups // 2
+
+    @pl.when(has_hi)
+    def _():
+        to_hi_aux.start()
+        for g in range(early):
+            to_hi(g).start()
+
+    @pl.when(has_lo)
+    def _():
+        to_lo_aux.start()
+        for g in range(early):
+            to_lo(g).start()
+
+    @pl.when(jnp.logical_not(has_lo))
+    def _():
+        bulk_lo[...] = jnp.zeros_like(bulk_lo)
+        aux_lo[...] = jnp.zeros_like(aux_lo)
+        he[0 : REACH * 8, :] = jnp.zeros((REACH * 8, lanes), jnp.float32)
+
+    @pl.when(jnp.logical_not(has_hi))
+    def _():
+        bulk_hi[...] = jnp.zeros_like(bulk_hi)
+        aux_hi[...] = jnp.zeros_like(aux_hi)
+        he[(REACH + rows) * 8 : hrows * 8, :] = jnp.zeros((REACH * 8, lanes), jnp.float32)
+
+    kb[REACH * 8 : (REACH + rows) * 8, :] = spread(ak[1])
+    def lon_sum(low, high):
+        total = pltpu.roll(low, REACH, 1) + pltpu.roll(high, lanes - REACH, 1)
+        for d in range(1, REACH):
+            total = total + (5.0 - d) * (pltpu.roll(low, d, 1) + pltpu.roll(high, lanes - d, 1))
+        return total
+
+    def lat_sum(ref, at):
+        total = ref[pl.ds(at - 8 * REACH, 64), :] + ref[pl.ds(at + 8 * REACH, 64), :]
+        for d in range(1, REACH):
+            total = total + (5.0 - d) * (
+                ref[pl.ds(at - 8 * d, 64), :] + ref[pl.ds(at + 8 * d, 64), :]
+            )
+        return total
+
+    weights = [
+        (
+            jnp.concatenate([jnp.where(lane >= d, 5.0 - d, 0.0)] * 8, axis=0),
+            jnp.concatenate([jnp.where(lane < lanes - d, 5.0 - d, 0.0)] * 8, axis=0),
+        )
+        for d in range(1, REACH + 1)
+    ]
+    at_edge = jnp.concatenate([(lane < REACH) | (lane >= lanes - REACH)] * 8, axis=0)
+    def place(sides, shift):
+        return jnp.where(at_edge, pltpu.roll(sides, shift, 1), 0.0)
+
+    def sweep(center, coeff, ref, at, edge):
+        along = lat_sum(ref, at)
+        for d in range(1, REACH + 1):
+            up, down = weights[d - 1]
+            along = along + up * pltpu.roll(center, d, 1) + down * pltpu.roll(center, lanes - d, 1)
+        along = 0.1 * along - 4.0 * center
+        if edge is not None:
+            along = along + edge
+        return center + coeff * along
+
+    def inside(g, carry):
+        base = g * erows * 8
+        for b in range(1, rows // 8):
+            at = pl.multiple_of(base + (REACH + 8 * b) * 8, 8)
+            one[pl.ds(pl.multiple_of(g * hrows * 8 + b * 64, 8), 64), :] = sweep(
+                ext[pl.ds(at, 64), :], kb[b * 64 : b * 64 + 64, :], ext, at, None
+            )
+        return carry
+
+    lax.fori_loop(0, groups, inside, 0)
+
+    to_right.wait()
+    to_left.wait()
+    low_side = lax.rem(lax.broadcasted_iota(jnp.int32, (64, lanes), 1), 16) < 8
+    for b in range(rows // 8):
+        he[(REACH + 8 * b) * 8 : (REACH + 8 * b + 8) * 8, :] = jnp.where(
+            low_side, px_left[b * 64 : b * 64 + 64, :], px_right[b * 64 : b * 64 + 64, :]
+        )
+    low_rows = lax.rem(lax.broadcasted_iota(jnp.int32, (rows, lanes), 1), 16) < 8
+    ko_side = jnp.where(
+        low_rows, px_left[rows * 8 : rows * 9, :], px_right[rows * 8 : rows * 9, :]
+    )
+    khb[...] = spread(ko_side)
+
+    cor_hi = remote(
+        he.at[rows * 8 : (rows + REACH) * 8, :], he.at[0 : REACH * 8, :],
+        cor_s.at[0], cor_r.at[0], {"lat": lat + 1},
+    )
+    cor_lo = remote(
+        he.at[REACH * 8 : 2 * REACH * 8, :], he.at[(REACH + rows) * 8 : hrows * 8, :],
+        cor_s.at[1], cor_r.at[1], {"lat": lat - 1},
+    )
+
+    @pl.when(has_hi)
+    def _():
+        cor_hi.start()
+        for g in range(early, groups):
+            to_hi(g).start()
+
+    @pl.when(has_lo)
+    def _():
+        cor_lo.start()
+        for g in range(early, groups):
+            to_lo(g).start()
 
     own_hab.wait()
     hf[...] = hb[...].astype(jnp.float32)
@@ -202,40 +283,6 @@
 
     lax.fori_loop(0, rows, likelihood, 0, unroll=2)
 
-    to_right.wait()
-    to_left.wait()
-    low_side = lax.rem(lax.broadcasted_iota(jnp.int32, (64, lanes), 1), 16) < 8
-    for b in range(rows // 8):
-        he[(REACH + 8 * b) * 8 : (REACH + 8 * b + 8) * 8, :] = jnp.where(
-            low_side, px_left[b * 64 : b * 64 + 64, :], px_right[b * 64 : b * 64 + 64, :]
-        )
-    low_rows = lax.rem(lax.broadcasted_iota(jnp.int32, (rows, lanes), 1), 16) < 8
-    ko_side = jnp.where(
-        low_rows, px_left[rows * 8 : rows * 9, :], px_right[rows * 8 : rows * 9, :]
-    )
-    khb[...] = spread(ko_side)
-
-    cor_hi = remote(
-        he.at[rows * 8 : (rows + REACH) * 8, :], he.at[0 : REACH * 8, :],
-        cor_s.at[0], cor_r.at[0], {"lat": lat + 1},
-    )
-    cor_lo = remote(
-        he.at[REACH * 8 : 2 * REACH * 8, :], he.at[(REACH + rows) * 8 : hrows * 8, :],
-        cor_s.at[1], cor_r.at[1], {"lat": lat - 1},
-    )
-
-    @pl.when(has_hi)
-    def _():
-        cor_hi.start()
-        for g in range(early, groups):
-            to_hi(g).start()
-
-    @pl.when(has_lo)
-    def _():
-        cor_lo.start()
-        for g in range(early, groups):
-            to_lo(g).start()
-
     @pl.when(has_lo)
     def _():
         to_hi_aux.wait_recv()
@@ -247,22 +294,7 @@
         cor_lo.wait_recv()
 
     kb[0 : REACH * 8, :] = spread(aux_lo[1])[REACH * 8 :]
-    kb[REACH * 8 : (REACH + rows) * 8, :] = spread(ak[1])
     kb[(REACH + rows) * 8 :, :] = spread(aux_hi[1])[: REACH * 8]
-
-    def lon_sum(low, high):
-        total = pltpu.roll(low, REACH, 1) + pltpu.roll(high, lanes - REACH, 1)
-        for d in range(1, REACH):
-            total = total + (5.0 - d) * (pltpu.roll(low, d, 1) + pltpu.roll(high, lanes - d, 1))
-        return total
-
-    def lat_sum(ref, at):
-        total = ref[pl.ds(at - 8 * REACH, 64), :] + ref[pl.ds(at + 8 * REACH, 64), :]
-        for d in range(1, REACH):
-            total = total + (5.0 - d) * (
-                ref[pl.ds(at - 8 * d, 64), :] + ref[pl.ds(at + 8 * d, 64), :]
-            )
-        return total
 
     def across(field):
         from_low = jnp.where(low_side, field, 0.0)
@@ -274,7 +306,7 @@
         return jnp.where(low_side, high, low)
 
     for b in range(hrows // 8):
-        ce[b * 64 : b * 64 + 64, :] = across(he[b * 64 : b * 64 + 64, :])
+        ce[b * 64 : b * 64 + 64, :] = 0.1 * across(he[b * 64 : b * 64 + 64, :])
 
     for b in range(rows // 8):
         at = (REACH + 8 * b) * 8
@@ -283,29 +315,14 @@
         z_left = jnp.where(low_side, side, inner)
         z_right = jnp.where(low_side, inner, side)
         along = jnp.where(low_side, lon_sum(z_left, z_left), lon_sum(z_right, z_right))
-        h1[b * 64 : b * 64 + 64, :] = across(
+        h1[b * 64 : b * 64 + 64, :] = 0.1 * across(
             side
             + khb[b * 64 : b * 64 + 64, :] * (0.1 * (along + lat_sum(he, at)) - 4.0 * side)
         )
 
-    weights = [
-        (
-            jnp.concatenate([jnp.where(lane >= d, 5.0 - d, 0.0)] * 8, axis=0),
-            jnp.concatenate([jnp.where(lane < lanes - d, 5.0 - d, 0.0)] * 8, axis=0),
-        )
-        for d in range(1, REACH + 1)
-    ]
-    at_edge = jnp.concatenate([(lane < REACH) | (lane >= lanes - REACH)] * 8, axis=0)
     low_flat = bulk_lo.reshape(tags * DEEP, lanes)
     high_flat = bulk_hi.reshape(tags * DEEP, lanes)
     acc[...] = jnp.zeros_like(acc)
-
-    def sweep(center, sides, shift, coeff, ref, at):
-        along = jnp.where(at_edge, pltpu.roll(sides, shift, 1), 0.0) + lat_sum(ref, at)
-        for d in range(1, REACH + 1):
-            up, down = weights[d - 1]
-            along = along + up * pltpu.roll(center, d, 1) + down * pltpu.roll(center, lanes - d, 1)
-        return center + coeff * (0.1 * along - 4.0 * center)
 
     def group(g, carry):
         @pl.when(has_lo)
@@ -325,28 +342,28 @@
                 pl.ds(g * 64 + a, 8, stride=DEEP), :
             ] * jnp.broadcast_to(aux_hi[0, a : a + 1, :], (8, lanes))
         shift = lax.rem(lanes - DEEP - 16 * g + lanes, lanes)
+        first_row = g * hrows * 8
         for b in range(hrows // 8):
             at = pl.multiple_of(base + (REACH + 8 * b) * 8, 8)
-            one[b * 64 : b * 64 + 64, :] = sweep(
-                ext[pl.ds(at, 64), :],
-                ce[b * 64 : b * 64 + 64, :],
-                shift,
-                kb[b * 64 : b * 64 + 64, :],
-                ext,
-                at,
-            )
+            there = pl.ds(pl.multiple_of(first_row + b * 64, 8), 64)
+            coeff = kb[b * 64 : b * 64 + 64, :]
+            edge = place(ce[b * 64 : b * 64 + 64, :], shift)
+            if 1 <= b < rows // 8:
+                one[there, :] = one[there, :] + coeff * edge
+            else:
+                one[there, :] = sweep(ext[pl.ds(at, 64), :], coeff, ext, at, edge)
         partial = jnp.zeros((8, lanes), jnp.float32)
         for b in range(rows // 8):
-            at = (REACH + 8 * b) * 8
+            start = (REACH + 8 * b) * 8
+            at = pl.multiple_of(first_row + start, 8)
             here = pl.ds(pl.multiple_of(g * rows * 8 + b * 64, 8), 64)
             updated = (
                 sweep(
-                    one[at : at + 64, :],
-                    h1[b * 64 : b * 64 + 64, :],
-                    shift,
-                    kb[at : at + 64, :],
+                    one[pl.ds(at, 64), :],
+                    kb[start : start + 64, :],
                     one,
                     at,
+                    place(h1[b * 64 : b * 64 + 64, :], shift),
                 )
                 * lik[here, :]
             )
@@ -446,7 +463,7 @@
             pltpu.VMEM((levels * rows, lanes), habitat.dtype),
             pltpu.VMEM((levels * rows, lanes), f32),
             pltpu.VMEM((groups * erows * 8, lanes), f32),
-            pltpu.VMEM((hrows * 8, lanes), f32),
+            pltpu.VMEM((groups * hrows * 8, lanes), f32),
             pltpu.VMEM((groups * rows * 8, lanes), f32),
             pltpu.VMEM((2, rows, lanes), f32),
             pltpu.VMEM((2, DEEP, lanes), f32),

time: 41.4 us -> 39 us (0.942)
  Pallas kernels: 37.8 us -> 35.3 us
    pallas_call x1, Pallas kernels: 37.8 us -> 35.3 us  [body(): pl.pallas_call(functools.partial(kernel, (n_lat, n_lon, tags, levels, row...]
where the time goes in v2:
time: 39 us; the launch traced here: 38.7 us
  Pallas kernels  35.3 us (91%)
  local copies, waits for them, and re-layouts  2.78 us (7%)
  between operations  0.65 us (2%)
    pallas_call x1, Pallas kernels, body(): pl.pallas_call(functools.partial(kernel, (n_lat, n_lon, tags, levels, row...  35.3 us
    unnamed x4, local copies, waits for them, and re-layouts  2.78 us

profile of v2, /device:TPU:0, one launch (start us, length us, event | category | flops | bytes accessed | tf_op | source)
XLA Modules:
  0.0 38.7 jit_solution(11517037514382251459)
XLA Ops:
  0.6 35.3 %filter_step.1 = (f32[2048,128]{1,0:T(8,128)}, f32[1,64]{1,0:T(1,128)}) custom-call(f32[64,32,128]{2,1,0:T(8,128)} %prior3.1, f32[2048,128]{1,0:T(8,128)} %bitcast.5, bf16[1024,128]{1,0:T(8,128)(2,1)} %bitcast.7, f32[32,128]{1,0:T(8,128)} %kappa.1, s32[32,128]{1,0:T(8,128)} %mask.1, f32[32,32]{1,0:T(8,128)} %profiles.1, s32[1,32]{1,0:T(1,128)} %bitcast.8), custom_call_target="tpu_custom_call" | custom-call | tf_op jit(solution)/shard_map/filter_step/pallas_call | solution.py:455
  35.9 0.0 copy-start
  35.9 2.3 %copy.10 = f32[64,32,128]{2,1,0:T(8,128)} copy(f32[64,32,128]{2,1,0:T(8,128)} %bitcast.6) | data formatting | bytes 2097152
  38.2 0.0 copy-done
  38.2 0.5 %copy.11 = f32[64]{0:T(128)} copy(f32[64]{0:T(128)S(1)} %bitcast.9) | data formatting | bytes 512
Async XLA Ops:
  35.9 2.3 %copy-start = (f32[1,64]{1,0:T(1,128)S(1)}, f32[1,64]{1,0:T(1,128)}, u32[]{:S(2)}) copy-start(f32[1,64]{1,0:T(1,128)} %get-tuple-element.5) | copy-start | bytes 772
